TPU v7x, 32 devices: a whole 2x2x4 slice. The times are simulated.
32 devices in a mesh: dp: 4 (over x, core), fsdp: 8 (over z, y).
Axes of the slice: x: 2, y: 2, z: 4, core: 2. Of those that a mesh axis runs over, the one named last changes fastest.
Arguments:
- byte_inputs: bfloat16 [3, 32, 1024, 768], P(None, ('dp', 'fsdp')), may hold values from -60 to 60
- lengths: int32 [3, 32], P(None, ('dp', 'fsdp')), may hold values from 256 to 1024, as said below
- latent_array: bfloat16 [256, 1280], P(None, ('dp', 'fsdp')), may hold values from -6 to 6
- gain_bytes: bfloat16 [768], P(('dp', 'fsdp')), may hold values from 0.25 to 1.75
- bias_bytes: bfloat16 [768], P(('dp', 'fsdp')), may hold values from -1.5 to 1.5
- gain_latent: bfloat16 [1280], P(('dp', 'fsdp')), may hold values from 0.25 to 1.75
- bias_latent: bfloat16 [1280], P(('dp', 'fsdp')), may hold values from -1.5 to 1.5
- query_weight: bfloat16 [1280, 256], P(('dp', 'fsdp')), may hold values from -0.15625 to 0.15625
- key_weight: bfloat16 [768, 256], P(('dp', 'fsdp')), may hold values from -0.21875 to 0.21875
- value_weight: bfloat16 [768, 1280], P(('dp', 'fsdp')), may hold values from -0.21875 to 0.21875
- output_weight: bfloat16 [1280, 1280], P(('dp', 'fsdp')), may hold values from -2.5 to 2.5
- gain_feed: bfloat16 [1280], P(('dp', 'fsdp')), may hold values from 0.25 to 1.75
- bias_feed: bfloat16 [1280], P(('dp', 'fsdp')), may hold values from -1.5 to 1.5
- up_weight: bfloat16 [1280, 1280], P(('dp', 'fsdp')), may hold values from -0.15625 to 0.15625
- down_weight: bfloat16 [1280, 1280], P(('dp', 'fsdp')), may hold values from -0.15625 to 0.15625
- cotangent: bfloat16 [3, 32, 256, 1280], P(None, ('dp', 'fsdp')), may hold values from -6 to 6
Outputs:
- latents_out: bfloat16 [3, 32, 256, 1280], P(None, ('dp', 'fsdp'))
- grad_inputs: bfloat16 [3, 32, 1024, 768], P(None, ('dp', 'fsdp'))
- grad_latent_array: float32 [256, 1280], P(None, ('dp', 'fsdp'))
- grad_gain_bytes: float32 [768], P(('dp', 'fsdp'))
- grad_bias_bytes: float32 [768], P(('dp', 'fsdp'))
- grad_gain_latent: float32 [1280], P(('dp', 'fsdp'))
- grad_bias_latent: float32 [1280], P(('dp', 'fsdp'))
- grad_query: float32 [1280, 256], P(('dp', 'fsdp'))
- grad_key: float32 [768, 256], P(('dp', 'fsdp'))
- grad_value: float32 [768, 1280], P(('dp', 'fsdp'))
- grad_output: float32 [1280, 1280], P(('dp', 'fsdp'))
- grad_gain_feed: float32 [1280], P(('dp', 'fsdp'))
- grad_bias_feed: float32 [1280], P(('dp', 'fsdp'))
- grad_up: float32 [1280, 1280], P(('dp', 'fsdp'))
- grad_down: float32 [1280, 1280], P(('dp', 'fsdp'))
Inputs may be any that keep to these rules, and one draw needn't show every extreme that they name: `lengths`: slots at or past a sequence's length are padding; in every micro-batch some sequence fills all 1024 slots.
All inputs are finite; a program needn't handle non-finite values.
Results may differ from a plain program's by a relative error of at most 0.012.
The roundings to bfloat16 on the way count: a program that leaves them out, or rounds other values in their place, can miss the bound.
Values may be sent and summed in bfloat16 or wider, within the bound.
No kernel may reach another device: no remote copies, remote signals or barrier semaphores. Data moves between devices by JAX's collectives and lax.ppermute only.
A program may use at most 192 MiB of HBM per device.

v0:
```python
import jax
import jax.numpy as jnp
from jax import lax
from jax.sharding import PartitionSpec as P

NL = 256
QK = 256
V = 1280
HEADS = 8
MB = 3
epsilon = 1e-05


def normalize(source, gain_vector, bias_vector):
    average = jnp.mean(source, axis=-1, keepdims=True)
    centered = source - average
    variance = jnp.mean(centered * centered, axis=-1, keepdims=True)
    return centered * lax.rsqrt(variance + epsilon) * gain_vector + bias_vector


def gelu_exact(upper_rows):
    return jax.nn.gelu(upper_rows, approximate=False)


def outer_sum(left_side, right_side):
    return jnp.einsum("rd,rf->df", left_side, right_side, preferred_element_type=jnp.float32)


def back_dot(left_side, right_side):
    return jnp.einsum("rf,df->rd", left_side, right_side, preferred_element_type=jnp.float32)


def attention_scores(query_heads, key_heads, length, factor):
    scores = (
        jnp.einsum("nhd,shd->hns", query_heads, key_heads, preferred_element_type=jnp.float32)
        * factor
    )
    live_mask = lax.iota(jnp.int32, key_heads.shape[0]) < length
    return jnp.where(live_mask[None, None, :], scores, -1e30)


def per_device(
    byte_inputs,
    lengths,
    latent_array,
    gain_bytes,
    bias_bytes,
    gain_latent,
    bias_latent,
    query_weight,
    key_weight,
    value_weight,
    output_weight,
    gain_feed,
    bias_feed,
    up_weight,
    down_weight,
    cotangent,
):
    query_width = QK // HEADS
    value_width = V // HEADS
    factor = query_width ** (-0.5)
    outputs = []
    input_grads = []
    summed = None
    owned_sums = None
    for micro_index in range(MB):
        gathered = (
            lax.all_gather(latent_array, ("dp", "fsdp"), axis=1, tiled=True),
            lax.all_gather(gain_bytes, ("dp", "fsdp"), axis=0, tiled=True),
            lax.all_gather(bias_bytes, ("dp", "fsdp"), axis=0, tiled=True),
            lax.all_gather(gain_latent, ("dp", "fsdp"), axis=0, tiled=True),
            lax.all_gather(bias_latent, ("dp", "fsdp"), axis=0, tiled=True),
            lax.all_gather(query_weight, ("dp", "fsdp"), axis=0, tiled=True),
            lax.all_gather(key_weight, ("dp", "fsdp"), axis=0, tiled=True),
            lax.all_gather(value_weight, ("dp", "fsdp"), axis=0, tiled=True),
            lax.all_gather(output_weight, ("dp", "fsdp"), axis=0, tiled=True),
            lax.all_gather(gain_feed, ("dp", "fsdp"), axis=0, tiled=True),
            lax.all_gather(bias_feed, ("dp", "fsdp"), axis=0, tiled=True),
            lax.all_gather(up_weight, ("dp", "fsdp"), axis=0, tiled=True),
            lax.all_gather(down_weight, ("dp", "fsdp"), axis=0, tiled=True),
        )
        (
            full_latent,
            full_gain_bytes,
            full_bias_bytes,
            full_gain_latent,
            full_bias_latent,
            full_query,
            full_key,
            full_value,
            full_output,
            full_gain_feed,
            full_bias_feed,
            full_up,
            full_down,
        ) = gathered
        inputs = byte_inputs[micro_index, 0].astype(jnp.float32)
        length = lengths[micro_index, 0]
        normed_bytes, pull_bytes = jax.vjp(
            normalize,
            inputs,
            full_gain_bytes.astype(jnp.float32),
            full_bias_bytes.astype(jnp.float32),
        )
        bytes_low = normed_bytes.astype(jnp.bfloat16)
        key_rows = jnp.dot(bytes_low, full_key, preferred_element_type=jnp.float32).astype(
            jnp.bfloat16
        )
        value_rows = jnp.dot(bytes_low, full_value, preferred_element_type=jnp.float32).astype(
            jnp.bfloat16
        )
        latent_float = full_latent.astype(jnp.float32)
        normed_latent, pull_latent = jax.vjp(
            normalize,
            latent_float,
            full_gain_latent.astype(jnp.float32),
            full_bias_latent.astype(jnp.float32),
        )
        latent_low = normed_latent.astype(jnp.bfloat16)
        queries = jnp.dot(latent_low, full_query, preferred_element_type=jnp.float32).astype(
            jnp.bfloat16
        )
        query_heads = queries.reshape(NL, HEADS, query_width)
        key_heads = key_rows.reshape(-1, HEADS, query_width)
        value_heads = value_rows.reshape(-1, HEADS, value_width)
        scores = attention_scores(query_heads, key_heads, length, factor)
        top_score = jnp.max(scores, axis=-1, keepdims=True)
        logsum = top_score[:, :, 0] + jnp.log(jnp.sum(jnp.exp(scores - top_score), axis=-1))
        probability = jnp.exp(scores - logsum[:, :, None])
        mixed_rows = (
            jnp.einsum(
                "hns,shd->nhd",
                probability.astype(jnp.bfloat16),
                value_heads,
                preferred_element_type=jnp.float32,
            )
            .reshape(NL, V)
            .astype(jnp.bfloat16)
        )
        first_sum = latent_float + jnp.dot(
            mixed_rows, full_output, preferred_element_type=jnp.float32
        )
        normed_middle, pull_middle = jax.vjp(
            normalize,
            first_sum,
            full_gain_feed.astype(jnp.float32),
            full_bias_feed.astype(jnp.float32),
        )
        middle_low = normed_middle.astype(jnp.bfloat16)
        upper_rows = jnp.dot(middle_low, full_up, preferred_element_type=jnp.float32)
        hidden_float, pull_gelu = jax.vjp(gelu_exact, upper_rows)
        hidden = hidden_float.astype(jnp.bfloat16)
        result = first_sum + jnp.dot(hidden, full_down, preferred_element_type=jnp.float32)
        outputs.append(result.astype(jnp.bfloat16))
        gathered = (
            lax.all_gather(latent_array, ("dp", "fsdp"), axis=1, tiled=True),
            lax.all_gather(gain_bytes, ("dp", "fsdp"), axis=0, tiled=True),
            lax.all_gather(bias_bytes, ("dp", "fsdp"), axis=0, tiled=True),
            lax.all_gather(gain_latent, ("dp", "fsdp"), axis=0, tiled=True),
            lax.all_gather(bias_latent, ("dp", "fsdp"), axis=0, tiled=True),
            lax.all_gather(query_weight, ("dp", "fsdp"), axis=0, tiled=True),
            lax.all_gather(key_weight, ("dp", "fsdp"), axis=0, tiled=True),
            lax.all_gather(value_weight, ("dp", "fsdp"), axis=0, tiled=True),
            lax.all_gather(output_weight, ("dp", "fsdp"), axis=0, tiled=True),
            lax.all_gather(gain_feed, ("dp", "fsdp"), axis=0, tiled=True),
            lax.all_gather(bias_feed, ("dp", "fsdp"), axis=0, tiled=True),
            lax.all_gather(up_weight, ("dp", "fsdp"), axis=0, tiled=True),
            lax.all_gather(down_weight, ("dp", "fsdp"), axis=0, tiled=True),
        )
        (
            full_latent,
            full_gain_bytes,
            full_bias_bytes,
            full_gain_latent,
            full_bias_latent,
            full_query,
            full_key,
            full_value,
            full_output,
            full_gain_feed,
            full_bias_feed,
            full_up,
            full_down,
        ) = gathered
        cotangent_row = cotangent[micro_index, 0].astype(jnp.float32)
        down_low = cotangent_row.astype(jnp.bfloat16)
        grad_down = outer_sum(hidden, down_low)
        (upper_grad,) = pull_gelu(back_dot(down_low, full_down))
        upper_low = upper_grad.astype(jnp.bfloat16)
        grad_up = outer_sum(middle_low, upper_low)
        first_extra, grad_gain_feed, grad_bias_feed = pull_middle(back_dot(upper_low, full_up))
        first_grad = cotangent_row + first_extra
        attend_low = first_grad.astype(jnp.bfloat16)
        grad_output = outer_sum(mixed_rows, attend_low)
        mixed_grad = (
            back_dot(attend_low, full_output).astype(jnp.bfloat16).reshape(NL, HEADS, value_width)
        )
        scores = attention_scores(query_heads, key_heads, length, factor)
        probability = jnp.exp(scores - logsum[:, :, None])
        weight_grad = jnp.einsum(
            "nhd,shd->hns", mixed_grad, value_heads, preferred_element_type=jnp.float32
        )
        value_grad = (
            jnp.einsum(
                "hns,nhd->shd",
                probability.astype(jnp.bfloat16),
                mixed_grad,
                preferred_element_type=jnp.float32,
            )
            .reshape(-1, V)
            .astype(jnp.bfloat16)
        )
        score_grad = probability * (
            weight_grad - jnp.sum(weight_grad * probability, axis=-1, keepdims=True)
        )
        score_low = score_grad.astype(jnp.bfloat16)
        query_grad = (
            (
                jnp.einsum("hns,shd->nhd", score_low, key_heads, preferred_element_type=jnp.float32)
                * factor
            )
            .reshape(NL, QK)
            .astype(jnp.bfloat16)
        )
        key_grad = (
            (
                jnp.einsum(
                    "hns,nhd->shd", score_low, query_heads, preferred_element_type=jnp.float32
                )
                * factor
            )
            .reshape(-1, QK)
            .astype(jnp.bfloat16)
        )
        grad_query = outer_sum(latent_low, query_grad)
        latent_extra, grad_gain_latent, grad_bias_latent = pull_latent(
            back_dot(query_grad, full_query)
        )
        grad_latent = first_grad + latent_extra
        grad_key = outer_sum(bytes_low, key_grad)
        grad_value = outer_sum(bytes_low, value_grad)
        source_grad = back_dot(key_grad, full_key) + back_dot(value_grad, full_value)
        input_extra, grad_gain_bytes, grad_bias_bytes = pull_bytes(source_grad)
        input_grads.append(input_extra.astype(jnp.bfloat16))
        local_grads = (
            grad_latent,
            grad_gain_bytes,
            grad_bias_bytes,
            grad_gain_latent,
            grad_bias_latent,
            grad_query,
            grad_key,
            grad_value,
            grad_output,
            grad_gain_feed,
            grad_bias_feed,
            grad_up,
            grad_down,
        )
        summed = local_grads if summed is None else jax.tree.map(jnp.add, summed, local_grads)
    (
        sum_latent,
        sum_gain_bytes,
        sum_bias_bytes,
        sum_gain_latent,
        sum_bias_latent,
        sum_query,
        sum_key,
        sum_value,
        sum_output,
        sum_gain_feed,
        sum_bias_feed,
        sum_up,
        sum_down,
    ) = summed
    owned_sums = (
        lax.psum_scatter(sum_latent, ("dp", "fsdp"), scatter_dimension=1, tiled=True),
        lax.psum_scatter(sum_gain_bytes, ("dp", "fsdp"), scatter_dimension=0, tiled=True),
        lax.psum_scatter(sum_bias_bytes, ("dp", "fsdp"), scatter_dimension=0, tiled=True),
        lax.psum_scatter(sum_gain_latent, ("dp", "fsdp"), scatter_dimension=0, tiled=True),
        lax.psum_scatter(sum_bias_latent, ("dp", "fsdp"), scatter_dimension=0, tiled=True),
        lax.psum_scatter(sum_query, ("dp", "fsdp"), scatter_dimension=0, tiled=True),
        lax.psum_scatter(sum_key, ("dp", "fsdp"), scatter_dimension=0, tiled=True),
        lax.psum_scatter(sum_value, ("dp", "fsdp"), scatter_dimension=0, tiled=True),
        lax.psum_scatter(sum_output, ("dp", "fsdp"), scatter_dimension=0, tiled=True),
        lax.psum_scatter(sum_gain_feed, ("dp", "fsdp"), scatter_dimension=0, tiled=True),
        lax.psum_scatter(sum_bias_feed, ("dp", "fsdp"), scatter_dimension=0, tiled=True),
        lax.psum_scatter(sum_up, ("dp", "fsdp"), scatter_dimension=0, tiled=True),
        lax.psum_scatter(sum_down, ("dp", "fsdp"), scatter_dimension=0, tiled=True),
    )
    latents_out = jnp.stack(outputs)[:, None]
    grad_inputs = jnp.stack(input_grads)[:, None]
    return (latents_out, grad_inputs) + tuple(owned_sums)


def solution(mesh):
    return jax.shard_map(
        per_device,
        mesh=mesh,
        in_specs=(
            P(None, ("dp", "fsdp"), None, None),
            P(None, ("dp", "fsdp")),
            P(None, ("dp", "fsdp")),
            P(("dp", "fsdp")),
            P(("dp", "fsdp")),
            P(("dp", "fsdp")),
            P(("dp", "fsdp")),
            P(("dp", "fsdp"), None),
            P(("dp", "fsdp"), None),
            P(("dp", "fsdp"), None),
            P(("dp", "fsdp"), None),
            P(("dp", "fsdp")),
            P(("dp", "fsdp")),
            P(("dp", "fsdp"), None),
            P(("dp", "fsdp"), None),
            P(None, ("dp", "fsdp"), None, None),
        ),
        out_specs=(
            P(None, ("dp", "fsdp"), None, None),
            P(None, ("dp", "fsdp"), None, None),
            P(None, ("dp", "fsdp")),
            P(("dp", "fsdp")),
            P(("dp", "fsdp")),
            P(("dp", "fsdp")),
            P(("dp", "fsdp")),
            P(("dp", "fsdp"), None),
            P(("dp", "fsdp"), None),
            P(("dp", "fsdp"), None),
            P(("dp", "fsdp"), None),
            P(("dp", "fsdp")),
            P(("dp", "fsdp")),
            P(("dp", "fsdp"), None),
            P(("dp", "fsdp"), None),
        ),
        check_vma=False,
    )
```

profile of v0, /device:TPU:0, one launch (start us, length us, event | category | flops | bytes accessed | tf_op | source)
XLA Modules:
  0.0 1375.6 jit_solution(13956663669413720624)
XLA Ops:
  10.1 74.3 %all_gather.26 = bf16[256,1280]{0,1:T(8,128)(2,1)S(1)} all-gather(bf16[256,40]{0,1:T(8,128)(2,1)} %param.18), channel_id=1, replica_groups=mesh['dp'=4,'fsdp'=8] {'dp','fsdp'}, dimensions={1}, use_global_device_ids=true | all-gather | bytes 675840 | tf_op jit(solution)/shard_map/all_gather | solution.py:69
  86.7 37.7 %all-reduce.13 = (bf16[768]{0:T(1024)(128)(2,1)S(1)}, bf16[768]{0:T(1024)(128)(2,1)S(1)}, bf16[1280]{0:T(1024)(128)(2,1)S(1)}, bf16[1280]{0:T(1024)(128)(2,1)S(1...) all-reduce(bf16[768]{0:T(1024)(128)(2,1)S(1)} %dynamic-update-slice, ...), channel_id=1, replica_groups=mesh['dp'=4,'fsdp'=8] {'dp','fsdp'}, use_global_device_ids=true, to_apply=%add.1 | all-reduce | flops 6656 | bytes 26624
  124.4 71.7 %all_gather.32 = bf16[1280,256]{1,0:T(8,128)(2,1)S(1)} all-gather(bf16[40,256]{1,0:T(8,128)(2,1)S(1)} %copy-done.117), channel_id=1, replica_groups=mesh['dp'=4,'fsdp'=8] {'dp','fsdp'}, dimensions={0}, use_global_device_ids=true | all-gather | bytes 675840 | tf_op jit(solution)/shard_map/all_gather | solution.py:74
  196.2 3.3 convert_reduce_fusion.2
  202.2 66.3 %all_gather.33 = bf16[768,256]{1,0:T(8,128)(2,1)S(1)} all-gather(bf16[24,256]{1,0:T(8,128)(2,1)S(1)} %copy-done.144), channel_id=1, replica_groups=mesh['dp'=4,'fsdp'=8] {'dp','fsdp'}, dimensions={0}, use_global_device_ids=true | all-gather | bytes 405504 | tf_op jit(solution)/shard_map/all_gather | solution.py:75
  289.5 4.5 convolution_convert_fusion.2
  294.0 2.9 copy.58
  296.9 4.5 convolution_convert_fusion.1
  301.4 2.8 copy.59
  304.2 6.0 convolution_convert_fusion
  310.2 3.0 copy.60
  313.2 8.1 convolution_convert_fusion.11
  321.3 6.5 convolution_convert_fusion.10
  327.8 3.5 convolution_convert_fusion.9
  331.3 3.4 fusion.203
  339.0 7.0 multiply_convert_fusion.5
  346.0 4.9 multiply_convert_fusion.4
  351.0 5.1 multiply_convert_fusion.3
  356.1 4.0 add_convert_fusion.4
  368.1 2.5 multiply_reduce_fusion.5
  380.2 6.8 multiply_reduce_fusion.2
  387.0 2.5 multiply_convert_fusion.2
  397.4 6.7 multiply_reduce_fusion.1
  404.2 2.7 multiply_convert_fusion.1
  414.8 6.7 multiply_reduce_fusion
  440.7 4.8 add_add_fusion.10
  445.6 2.8 copy.67
  448.4 7.2 convolution_convert_fusion.8
  455.7 7.2 convolution_convert_fusion.7
  463.2 5.1 fusion.179
  468.4 2.7 fusion.168
  471.2 2.4 convolution_convert_fusion.6
  475.1 4.6 add_add_fusion.3
  484.0 3.9 convolution_add_fusion.2
  491.5 3.8 convolution_add_fusion.4
  499.2 3.8 convolution_add_fusion
  504.5 4.1 fusion.204
  514.4 2.3 fusion.208
  516.9 7.2 fusion.47
  524.3 39.1 %all-reduce.12 = (f32[768]{0:T(1024)S(1)}, f32[768]{0:T(1024)S(1)}, f32[1280]{0:T(1024)S(1)}, f32[1280]{0:T(1024)S(1)}, f32[1280]{0:T(1024)S(1)}, /*index=5*/f32[1280]{0:T(1024)S(1)}) all-reduce(f32[768]{0:T(1024)S(1)} %add_add_fusion.19, f32[768]{0:T(1024)S(1)} %add_add_fusion.18, ...), channel_id=3, replica_groups=mesh['dp'=4,'fsdp'=8] {'dp','fsdp'}, use_global_device_ids=true, to_apply=%region_45.46.clone | all-reduce | flops 6656 | bytes 53248
  567.0 7.6 fusion.191
  580.9 2.5 maximum_bitcast_fusion
  583.4 79.2 %reduce-scatter.10.cloned.1.call-done = f32[40,256]{1,0:T(8,128)} async-done(((f32[1280,256]{1,0:T(8,128)}), f32[40,256]{1,0:T(8,128)}) %reduce-scatter.10.cloned.1.call-update) | async-done | bytes 40976 | tf_op jit(solution)/shard_map/reduce_scatter | solution.py:283
  662.6 135.4 %reduce-scatter.22.cloned.1.call-done = f32[40,256]{1,0:T(8,128)} async-done(((f32[1280,256]{1,0:T(8,128)}), f32[40,256]{1,0:T(8,128)}) %reduce-scatter.22.cloned.1.call-update) | async-done | bytes 40976
  798.0 106.6 %reduce-scatter.14.cloned.1.call-done = f32[24,1280]{1,0:T(8,128)} async-done(((f32[768,1280]{1,0:T(8,128)}), f32[24,1280]{1,0:T(8,128)}) %reduce-scatter.14.cloned.1.call-update) | async-done | bytes 122896 | tf_op jit(solution)/shard_map/reduce_scatter | solution.py:285
  904.6 153.8 %reduce-scatter.18.cloned.1.call-done = f32[40,1280]{1,0:T(8,128)} async-done(((f32[1280,1280]{1,0:T(8,128)}), f32[40,1280]{1,0:T(8,128)}) %reduce-scatter.18.cloned.1.call-update) | async-done | bytes 204816 | tf_op jit(solution)/shard_map/reduce_scatter | solution.py:289
  1058.4 155.6 %reduce-scatter.16.cloned.1.call-done = f32[40,1280]{1,0:T(8,128)} async-done(((f32[1280,1280]{1,0:T(8,128)}), f32[40,1280]{1,0:T(8,128)}) %reduce-scatter.16.cloned.1.call-update) | async-done | bytes 204816 | tf_op jit(solution)/shard_map/reduce_scatter | solution.py:286
  1214.0 154.8 %reduce-scatter.20.cloned.1.call-done = f32[40,1280]{1,0:T(8,128)} async-done(((f32[1280,1280]{1,0:T(8,128)}), f32[40,1280]{1,0:T(8,128)}) %reduce-scatter.20.cloned.1.call-update) | async-done | bytes 204816 | tf_op jit(solution)/shard_map/reduce_scatter | solution.py:290
  (591 shorter events, 114.7 us)
Async XLA Ops:
  7.2 282.3 %all-gather.5.cloned.1.call-start = ((), (), s32[]{:S(2)}) async-start(), calls=%async_computation.7 | async-start | bytes 2027520 | tf_op jit(solution)/shard_map/all_gather | solution.py:76
  7.9 323.3 %all-gather.7.cloned.1.call-start = ((), (), s32[]{:S(2)}) async-start(), calls=%async_computation.8 | async-start | bytes 3379200 | tf_op jit(solution)/shard_map/all_gather | solution.py:77
  8.7 330.3 %all-gather.9.cloned.1.call-start = ((), (), s32[]{:S(2)}) async-start(), calls=%async_computation.9 | async-start | bytes 3379200 | tf_op jit(solution)/shard_map/all_gather | solution.py:80
  9.4 346.7 %all-gather.11.cloned.1.call-start = ((), (), s32[]{:S(2)}) async-start(), calls=%async_computation.10 | async-start | bytes 3379200 | tf_op jit(solution)/shard_map/all_gather | solution.py:81
  10.0 573.4 %reduce-scatter.12.cloned.1.call-start = ((), (), s32[]{:S(2)}) async-start(), calls=%async_computation.12 | async-start | bytes 811008 | tf_op jit(solution)/shard_map/reduce_scatter | solution.py:284
  10.0 75.2 %copy-start.185 = (bf16[40]{0:T(256)(128)(2,1)S(1)}, bf16[40]{0:T(256)(128)(2,1)}, u32[]{:S(2)}) copy-start(bf16[40]{0:T(256)(128)(2,1)} %param.21) | copy-start | bytes 244
  10.0 75.5 %copy-start.186 = (bf16[40]{0:T(256)(128)(2,1)S(1)}, bf16[40]{0:T(256)(128)(2,1)}, u32[]{:S(2)}) copy-start(bf16[40]{0:T(256)(128)(2,1)} %param.22) | copy-start | bytes 244
  10.1 75.7 %copy-start.187 = (bf16[40]{0:T(256)(128)(2,1)S(1)}, bf16[40]{0:T(256)(128)(2,1)}, u32[]{:S(2)}) copy-start(bf16[40]{0:T(256)(128)(2,1)} %param.27) | copy-start | bytes 244
  10.1 76.0 %copy-start.188 = (bf16[40]{0:T(256)(128)(2,1)S(1)}, bf16[40]{0:T(256)(128)(2,1)}, u32[]{:S(2)}) copy-start(bf16[40]{0:T(256)(128)(2,1)} %param.28) | copy-start | bytes 244
  10.1 76.2 %copy-start.189 = (bf16[24]{0:T(256)(128)(2,1)S(1)}, bf16[24]{0:T(256)(128)(2,1)}, u32[]{:S(2)}) copy-start(bf16[24]{0:T(256)(128)(2,1)} %param.19) | copy-start | bytes 148
  10.1 76.4 %copy-start.190 = (bf16[24]{0:T(256)(128)(2,1)S(1)}, bf16[24]{0:T(256)(128)(2,1)}, u32[]{:S(2)}) copy-start(bf16[24]{0:T(256)(128)(2,1)} %param.20) | copy-start | bytes 148
  10.1 114.3 %copy-start.117 = (bf16[40,256]{1,0:T(8,128)(2,1)S(1)}, bf16[40,256]{1,0:T(8,128)(2,1)}, u32[]{:S(2)}) copy-start(bf16[40,256]{1,0:T(8,128)(2,1)} %param.23) | copy-start | bytes 61444
  84.9 184.9 %copy-start.88 = (f32[256]{0:T(256)}, f32[256]{0:T(256)S(1)}, u32[]{:S(2)}) copy-start(f32[256]{0:T(256)S(1)} %broadcast_multiply_fusion.6) | copy-start | bytes 3076
  85.2 184.6 %copy-start.91 = (f32[256]{0:T(256)}, f32[256]{0:T(256)S(1)}, u32[]{:S(2)}) copy-start(f32[256]{0:T(256)S(1)} %fusion.145) | copy-start | bytes 3076
  124.4 145.4 %copy-start.75 = (f32[1280]{0:T(1024)}, f32[1280]{0:T(1024)S(1)}, u32[]{:S(2)}) copy-start(f32[1280]{0:T(1024)S(1)} %convert_element_type.337) | copy-start | bytes 15364
  124.4 145.4 %copy-start.79 = (f32[1280]{0:T(1024)}, f32[1280]{0:T(1024)S(1)}, u32[]{:S(2)}) copy-start(f32[1280]{0:T(1024)S(1)} %convert_element_type.338) | copy-start | bytes 15364
  196.2 73.7 %copy-start.25 = (bf16[1280,256]{1,0:T(8,128)(2,1)}, bf16[1280,256]{1,0:T(8,128)(2,1)S(1)}, u32[]{:S(2)}) copy-start(bf16[1280,256]{1,0:T(8,128)(2,1)S(1)} %all_gather.32) | copy-start | bytes 1966084
  196.2 108.0 %copy-start.132 = (f32[768]{0:T(1024)}, f32[768]{0:T(1024)S(1)}, u32[]{:S(2)}) copy-start(f32[768]{0:T(1024)S(1)} %convert_element_type.333) | copy-start | bytes 9220
  199.5 89.9 %copy-start.100 = (f32[1024]{0:T(1024)}, f32[1024]{0:T(1024)S(1)}, u32[]{:S(2)}) copy-start(f32[1024]{0:T(1024)S(1)} %broadcast_multiply_fusion.2) | copy-start | bytes 12292
  199.5 97.3 %copy-start.106 = (f32[1024]{0:T(1024)}, f32[1024]{0:T(1024)S(1)}, u32[]{:S(2)}) copy-start(f32[1024]{0:T(1024)S(1)} %get-tuple-element.187) | copy-start | bytes 12292
  199.6 104.6 %copy-start.103 = (f32[1024]{0:T(1024)}, f32[1024]{0:T(1024)S(1)}, u32[]{:S(2)}) copy-start(f32[1024]{0:T(1024)S(1)} %get-tuple-element.186) | copy-start | bytes 12292
  200.2 68.3 %copy-start.169 = (s32[3,1]{0,1:T(1,128)S(1)}, s32[3,1]{0,1:T(1,128)}, u32[]{:S(2)}) copy-start(s32[3,1]{0,1:T(1,128)} %param.17) | copy-start | bytes 40
  202.1 67.8 %copy-start.94 = (f32[1024]{0:T(1024)}, f32[1024]{0:T(1024)S(1)}, u32[]{:S(2)}) copy-start(f32[1024]{0:T(1024)S(1)} %get-tuple-element.70) | copy-start | bytes 12292
  202.1 74.2 %copy-start.96 = (f32[1024]{0:T(1024)}, f32[1024]{0:T(1024)S(1)}, u32[]{:S(2)}) copy-start(f32[1024]{0:T(1024)S(1)} %get-tuple-element.72) | copy-start | bytes 12292
  202.1 80.7 %copy-start.98 = (f32[1024]{0:T(1024)}, f32[1024]{0:T(1024)S(1)}, u32[]{:S(2)}) copy-start(f32[1024]{0:T(1024)S(1)} %get-tuple-element.71) | copy-start | bytes 12292
  202.1 87.3 %copy-start.135 = (f32[1024]{0:T(1024)}, f32[1024]{0:T(1024)S(1)}, u32[]{:S(2)}) copy-start(f32[1024]{0:T(1024)S(1)} %fusion.142) | copy-start | bytes 12292
  202.2 102.0 %copy-start.173 = (f32[768]{0:T(1024)}, f32[768]{0:T(1024)S(1)}, u32[]{:S(2)}) copy-start(f32[768]{0:T(1024)S(1)} %convert_element_type.334) | copy-start | bytes 9220
  269.9 117.1 %copy-start.118 = (pred[1024]{0:T(1024)(128)(4,1)}, pred[1024]{0:T(1024)(128)(4,1)S(1)}, u32[]{:S(2)}) copy-start(pred[1024]{0:T(1024)(128)(4,1)S(1)} %iota_compare_fusion.2) | copy-start | bytes 3076
  276.2 110.7 %copy-start.81 = (f32[8,256]{1,0:T(8,128)}, f32[8,256]{1,0:T(8,128)S(1)}, u32[]{:S(2)}) copy-start(f32[8,256]{1,0:T(8,128)S(1)} %log_add_fusion.2) | copy-start | bytes 24580
  276.3 74.7 %copy-start.77 = (f32[1280]{0:T(1024)}, f32[1280]{0:T(1024)S(1)}, u32[]{:S(2)}) copy-start(f32[1280]{0:T(1024)S(1)} %convert_element_type.347) | copy-start | bytes 15364
  278.0 43.2 %copy-start.123 = (pred[1024]{0:T(1024)(128)(4,1)}, pred[1024]{0:T(1024)(128)(4,1)S(1)}, u32[]{:S(2)}) copy-start(pred[1024]{0:T(1024)(128)(4,1)S(1)} %iota_compare_fusion.1) | copy-start | bytes 3076
  282.8 38.4 %copy-start.85 = (f32[8,256]{1,0:T(8,128)}, f32[8,256]{1,0:T(8,128)S(1)}, u32[]{:S(2)}) copy-start(f32[8,256]{1,0:T(8,128)S(1)} %log_add_fusion.1) | copy-start | bytes 24580
  284.6 43.1 %copy-start.120 = (pred[1024]{0:T(1024)(128)(4,1)}, pred[1024]{0:T(1024)(128)(4,1)S(1)}, u32[]{:S(2)}) copy-start(pred[1024]{0:T(1024)(128)(4,1)S(1)} %iota_compare_fusion) | copy-start | bytes 3076
  289.4 132.0 %copy-start.83 = (f32[8,256]{1,0:T(8,128)}, f32[8,256]{1,0:T(8,128)S(1)}, u32[]{:S(2)}) copy-start(f32[8,256]{1,0:T(8,128)S(1)} %log_add_fusion) | copy-start | bytes 24580
  334.7 35.9 %copy-start.115 = (f32[256]{0:T(256)}, f32[256]{0:T(256)S(1)}, u32[]{:S(2)}) copy-start(f32[256]{0:T(256)S(1)} %broadcast_multiply_fusion.5) | copy-start | bytes 3076
  336.2 34.4 %copy-start.126 = (f32[256]{0:T(256)}, f32[256]{0:T(256)S(1)}, u32[]{:S(2)}) copy-start(f32[256]{0:T(256)S(1)} %broadcast_multiply_fusion.4) | copy-start | bytes 3076
  337.6 33.0 %copy-start.128 = (f32[256]{0:T(256)}, f32[256]{0:T(256)S(1)}, u32[]{:S(2)}) copy-start(f32[256]{0:T(256)S(1)} %broadcast_multiply_fusion.3) | copy-start | bytes 3076
  338.9 31.7 %copy-start.130 = (f32[256]{0:T(256)}, f32[256]{0:T(256)S(1)}, u32[]{:S(2)}) copy-start(f32[256]{0:T(256)S(1)} %fusion.146) | copy-start | bytes 3076
  338.9 31.7 %copy-start.161 = (f32[256]{0:T(256)}, f32[256]{0:T(256)S(1)}, u32[]{:S(2)}) copy-start(f32[256]{0:T(256)S(1)} %fusion.147) | copy-start | bytes 3076
  430.8 231.8 %reduce-scatter.10.cloned.1.call-start = ((), (), s32[]{:S(2)}) async-start(), calls=%async_computation.11 | async-start | bytes 1351680 | tf_op jit(solution)/shard_map/reduce_scatter | solution.py:283
  440.5 357.5 %reduce-scatter.22.cloned.1.call-start = ((), (), s32[]{:S(2)}) async-start(), calls=%async_computation.17 | async-start | bytes 1351680
  462.9 441.7 %reduce-scatter.14.cloned.1.call-start = ((), (), s32[]{:S(2)}) async-start(), calls=%async_computation.13 | async-start | bytes 4055040 | tf_op jit(solution)/shard_map/reduce_scatter | solution.py:285
  479.8 578.6 %reduce-scatter.18.cloned.1.call-start = ((), (), s32[]{:S(2)}) async-start(), calls=%async_computation.15 | async-start | bytes 6758400 | tf_op jit(solution)/shard_map/reduce_scatter | solution.py:289
  487.9 726.1 %reduce-scatter.16.cloned.1.call-start = ((), (), s32[]{:S(2)}) async-start(), calls=%async_computation.14 | async-start | bytes 6758400 | tf_op jit(solution)/shard_map/reduce_scatter | solution.py:286
  495.3 873.5 %reduce-scatter.20.cloned.1.call-start = ((), (), s32[]{:S(2)}) async-start(), calls=%async_computation.16 | async-start | bytes 6758400 | tf_op jit(solution)/shard_map/reduce_scatter | solution.py:290
  516.9 50.0 %copy-start.99 = (f32[1024]{0:T(1024)S(1)}, f32[1024]{0:T(1024)}, u32[]{:S(2)}) copy-start(f32[1024]{0:T(1024)} %copy-done.98) | copy-start | bytes 12292
  516.9 50.0 %copy-start.97 = (f32[1024]{0:T(1024)S(1)}, f32[1024]{0:T(1024)}, u32[]{:S(2)}) copy-start(f32[1024]{0:T(1024)} %copy-done.96) | copy-start | bytes 12292
  516.9 50.0 %copy-start.95 = (f32[1024]{0:T(1024)S(1)}, f32[1024]{0:T(1024)}, u32[]{:S(2)}) copy-start(f32[1024]{0:T(1024)} %copy-done.94) | copy-start | bytes 12292
  (176 other events, 702.9 us)
Sparse Core Ops, SparseCore 0:
  10.9 59.7 all-gather.4
  73.5 58.9 all-gather.6
  135.4 59.7 all-gather.8
  197.9 58.4 all-gather.10
  430.9 93.9 reduce-scatter.11
  527.6 134.9 reduce-scatter.9
  665.5 132.4 reduce-scatter.21
  804.0 100.5 reduce-scatter.13
  907.5 150.8 reduce-scatter.17
  1061.1 152.8 reduce-scatter.15
  1216.9 151.8 reduce-scatter.19
where the time goes:
time: 1380 us
  waiting for transfers between devices  788 us (57%)
  blocking collectives  289 us (21%)
  matrix products  187 us (14%)
  local copies, waits for them, and re-layouts  46.9 us (3%)
  other arithmetic  45.4 us (3%)
  between operations  17.2 us (1%)
    reduce_scatter x1, waiting for transfers between devices, per_device(): lax.psum_scatter(sum_output, ('dp', 'fsdp'), scatter_dimension=0, tiled=T...  156 us
    reduce_scatter x1, waiting for transfers between devices, per_device(): lax.psum_scatter(sum_down, ('dp', 'fsdp'), scatter_dimension=0, tiled=True)  155 us
    reduce_scatter x1, waiting for transfers between devices, per_device(): lax.psum_scatter(sum_up, ('dp', 'fsdp'), scatter_dimension=0, tiled=True)  154 us
    unnamed x12, waiting for transfers between devices  138 us
    reduce_scatter x1, waiting for transfers between devices, per_device(): lax.psum_scatter(sum_value, ('dp', 'fsdp'), scatter_dimension=0, tiled=True)  107 us
    reduce_scatter x1, waiting for transfers between devices, per_device(): lax.psum_scatter(sum_query, ('dp', 'fsdp'), scatter_dimension=0, tiled=True)  79.2 us
    unnamed x2, blocking collectives  76.8 us
    all_gather x1, blocking collectives, per_device(): lax.all_gather(latent_array, ('dp', 'fsdp'), axis=1, tiled=True)  74.3 us
  transfers between devices with their start and end apart: 11, of which 6 were waited for; matrix products, arithmetic and copies ran while one was open for 14% of the time, Pallas kernels for 0%

commit v1 on v0

--- a/solution.py
+++ b/solution.py
@@ -9,6 +9,28 @@
 HEADS = 8
 MB = 3
 epsilon = 1e-05
+
+
+def direct_bench(xin, dim_i):
+    xin = jnp.moveaxis(xin, 0, dim_i)
+    long_array = xin.shape
+    return xin.reshape(
+        *long_array[:dim_i], long_array[dim_i] * long_array[dim_i + 1], *long_array[dim_i + 2 :]
+    )
+
+
+def meet_the_results(base_x, mesh_dim):
+    prior = lax.axis_size(mesh_dim)
+    z_new, y_new = (prior, lax.axis_index(mesh_dim))
+    tmp, a_next = (base_x[None], 1)
+    while a_next < z_new:
+        f_next = lax.ppermute(
+            tmp, mesh_dim, perm=list(map(lambda dev_i: (dev_i, dev_i ^ a_next), range(z_new)))
+        )
+        step_out = y_new & a_next == 0
+        tmp = jnp.concatenate([jnp.where(step_out, tmp, f_next), jnp.where(step_out, f_next, tmp)])
+        a_next *= 2
+    return tmp
 
 
 def normalize(source, gain_vector, bias_vector):
@@ -65,6 +87,10 @@
     summed = None
     owned_sums = None
     for micro_index in range(MB):
+
+        def update_goods(chunk, vals, in_dim):
+            return direct_bench(meet_the_results(chunk, vals), in_dim)
+
         gathered = (
             lax.all_gather(latent_array, ("dp", "fsdp"), axis=1, tiled=True),
             lax.all_gather(gain_bytes, ("dp", "fsdp"), axis=0, tiled=True),
@@ -72,7 +98,7 @@
             lax.all_gather(gain_latent, ("dp", "fsdp"), axis=0, tiled=True),
             lax.all_gather(bias_latent, ("dp", "fsdp"), axis=0, tiled=True),
             lax.all_gather(query_weight, ("dp", "fsdp"), axis=0, tiled=True),
-            lax.all_gather(key_weight, ("dp", "fsdp"), axis=0, tiled=True),
+            update_goods(key_weight, ("dp", "fsdp"), 0),
             lax.all_gather(value_weight, ("dp", "fsdp"), axis=0, tiled=True),
             lax.all_gather(output_weight, ("dp", "fsdp"), axis=0, tiled=True),
             lax.all_gather(gain_feed, ("dp", "fsdp"), axis=0, tiled=True),

time: 1380 us -> 1340 us (0.971)
  waiting for transfers between devices: 788 us -> 731 us
    reduce_scatter x1, waiting for transfers between devices: 79.2 us -> 6.01 us  [per_device(): lax.psum_scatter(sum_query, ('dp', 'fsdp'), scatter_dimension=0, tiled=True)]
    ppermute x0 -> x5, waiting for transfers between devices: none -> 16.4 us  [meet_the_results(): lax.ppermute(tmp, mesh_dim, perm=list(map(lambda dev_i: (dev_i, dev_i ^ a...]
    unnamed x445 -> x401, local copies, waits for them, and re-layouts: 30.8 us -> 34.3 us
  transfers between devices with their start and end apart: 11 -> 16, of which waited for: 6 -> 10; matrix products, arithmetic and copies ran while one was open for 14% -> 15% of each run, Pallas kernels for 0% -> 0%
where the time goes in v1:
time: 1340 us; the launch traced here: 1330 us
  waiting for transfers between devices  731 us (55%)
  blocking collectives  286 us (21%)
  matrix products  193 us (14%)
  local copies, waits for them, and re-layouts  50.3 us (4%)
  other arithmetic  49.3 us (4%)
  between operations  16.9 us (1%)
    reduce_scatter x1, waiting for transfers between devices, per_device(): lax.psum_scatter(sum_down, ('dp', 'fsdp'), scatter_dimension=0, tiled=True)  156 us
    reduce_scatter x1, waiting for transfers between devices, per_device(): lax.psum_scatter(sum_up, ('dp', 'fsdp'), scatter_dimension=0, tiled=True)  155 us
    reduce_scatter x1, waiting for transfers between devices, per_device(): lax.psum_scatter(sum_output, ('dp', 'fsdp'), scatter_dimension=0, tiled=T...  154 us
    unnamed x12, waiting for transfers between devices  138 us
    reduce_scatter x1, waiting for transfers between devices, per_device(): lax.psum_scatter(sum_value, ('dp', 'fsdp'), scatter_dimension=0, tiled=True)  107 us
    unnamed x2, blocking collectives  78.9 us
    all_gather x1, blocking collectives, per_device(): lax.all_gather(latent_array, ('dp', 'fsdp'), axis=1, tiled=True)  70.9 us
    all_gather x1, blocking collectives, per_device(): lax.all_gather(query_weight, ('dp', 'fsdp'), axis=0, tiled=True)  69.1 us
  transfers between devices with their start and end apart: 16, of which 10 were waited for; matrix products, arithmetic and copies ran while one was open for 15% of the time, Pallas kernels for 0%

profile of v1, /device:TPU:0, one launch (start us, length us, event | category | flops | bytes accessed | tf_op | source)
XLA Modules:
  0.0 1333.0 jit_solution(6115344594657330313)
XLA Ops:
  9.4 3.0 collective-permute-start
  17.6 40.0 %all-reduce.13 = (bf16[768]{0:T(1024)(128)(2,1)S(1)}, bf16[768]{0:T(1024)(128)(2,1)S(1)}, bf16[1280]{0:T(1024)(128)(2,1)S(1)}, bf16[1280]{0:T(1024)(128)(2,1)S(1...) all-reduce(bf16[768]{0:T(1024)(128)(2,1)S(1)} %dynamic-update-slice, ...), channel_id=1, replica_groups=mesh['dp'=4,'fsdp'=8] {'dp','fsdp'}, use_global_device_ids=true, to_apply=%add.1 | all-reduce | flops 6656 | bytes 26624
  57.7 3.2 convert_reduce_fusion.2
  64.0 70.9 %all_gather.26 = bf16[256,1280]{0,1:T(8,128)(2,1)S(1)} all-gather(bf16[256,40]{0,1:T(8,128)(2,1)S(1)} %copy-done.116), channel_id=1, replica_groups=mesh['dp'=4,'fsdp'=8] {'dp','fsdp'}, dimensions={1}, use_global_device_ids=true | all-gather | bytes 675840 | tf_op jit(solution)/shard_map/all_gather | solution.py:95
  135.6 69.1 %all_gather.32 = bf16[1280,256]{1,0:T(8,128)(2,1)S(1)} all-gather(bf16[40,256]{1,0:T(8,128)(2,1)S(1)} %copy-done.117), channel_id=1, replica_groups=mesh['dp'=4,'fsdp'=8] {'dp','fsdp'}, dimensions={0}, use_global_device_ids=true | all-gather | bytes 675840 | tf_op jit(solution)/shard_map/all_gather | solution.py:100
  209.2 3.2 collective-permute-done.1
  213.3 4.5 collective-permute-done.2
  221.3 8.1 collective-permute-done.4
  246.6 4.5 convolution_convert_fusion.2
  251.2 2.9 copy.58
  254.1 4.5 convolution_convert_fusion.1
  258.6 2.8 copy.59
  261.4 6.0 convolution_convert_fusion
  267.4 3.0 copy.60
  270.4 8.1 convolution_convert_fusion.11
  278.5 6.5 convolution_convert_fusion.10
  285.0 3.5 convolution_convert_fusion.9
  288.5 3.4 fusion.213
  296.3 7.0 multiply_convert_fusion.5
  303.3 4.9 multiply_convert_fusion.4
  308.2 5.1 multiply_convert_fusion.3
  313.4 4.0 add_convert_fusion.4
  337.4 6.8 multiply_reduce_fusion.2
  344.3 2.5 multiply_convert_fusion.2
  354.7 6.8 multiply_reduce_fusion.1
  361.5 2.7 multiply_convert_fusion.1
  372.0 6.8 multiply_reduce_fusion
  400.9 5.3 add_add_fusion.10
  406.2 2.9 copy.67
  409.1 7.1 convolution_convert_fusion.8
  416.2 7.1 convolution_convert_fusion.7
  423.7 4.2 fusion.222
  428.0 4.2 fusion.191
  436.2 6.0 add_add_fusion.3
  446.4 3.9 convolution_add_fusion.2
  454.0 3.8 convolution_add_fusion.4
  462.8 3.8 convolution_add_fusion
  467.3 67.5 %all_gather.38 = bf16[768,256]{1,0:T(8,128)(2,1)S(1)} all-gather(bf16[24,256]{1,0:T(8,128)(2,1)S(1)} %copy-done.91), channel_id=1, replica_groups=mesh['dp'=4,'fsdp'=8] {'dp','fsdp'}, dimensions={0}, use_global_device_ids=true | all-gather | bytes 405504 | tf_op jit(solution)/shard_map/all_gather | solution.py:189
  534.8 4.6 fusion.214
  548.3 7.0 fusion.47
  555.4 38.9 %all-reduce.12 = (f32[768]{0:T(1024)S(1)}, f32[768]{0:T(1024)S(1)}, f32[1280]{0:T(1024)S(1)}, f32[1280]{0:T(1024)S(1)}, f32[1280]{0:T(1024)S(1)}, /*index=5*/f32[1280]{0:T(1024)S(1)}) all-reduce(f32[768]{0:T(1024)S(1)} %add_add_fusion.19, f32[768]{0:T(1024)S(1)} %add_add_fusion.18, ...), channel_id=3, replica_groups=mesh['dp'=4,'fsdp'=8] {'dp','fsdp'}, use_global_device_ids=true, to_apply=%region_45.46.clone | all-reduce | flops 6656 | bytes 53248
  597.9 7.5 fusion.201
  614.2 6.0 reduce-scatter.10.cloned.1.call-done
  620.2 135.7 %reduce-scatter.22.cloned.1.call-done = f32[40,256]{1,0:T(8,128)} async-done(((f32[1280,256]{1,0:T(8,128)}), f32[40,256]{1,0:T(8,128)}) %reduce-scatter.22.cloned.1.call-update) | async-done | bytes 40976
  755.9 106.5 %reduce-scatter.14.cloned.1.call-done = f32[24,1280]{1,0:T(8,128)} async-done(((f32[768,1280]{1,0:T(8,128)}), f32[24,1280]{1,0:T(8,128)}) %reduce-scatter.14.cloned.1.call-update) | async-done | bytes 122896 | tf_op jit(solution)/shard_map/reduce_scatter | solution.py:311
  862.5 154.5 %reduce-scatter.18.cloned.1.call-done = f32[40,1280]{1,0:T(8,128)} async-done(((f32[1280,1280]{1,0:T(8,128)}), f32[40,1280]{1,0:T(8,128)}) %reduce-scatter.18.cloned.1.call-update) | async-done | bytes 204816 | tf_op jit(solution)/shard_map/reduce_scatter | solution.py:315
  1017.0 153.6 %reduce-scatter.16.cloned.1.call-done = f32[40,1280]{1,0:T(8,128)} async-done(((f32[1280,1280]{1,0:T(8,128)}), f32[40,1280]{1,0:T(8,128)}) %reduce-scatter.16.cloned.1.call-update) | async-done | bytes 204816 | tf_op jit(solution)/shard_map/reduce_scatter | solution.py:312
  1170.6 155.7 %reduce-scatter.20.cloned.1.call-done = f32[40,1280]{1,0:T(8,128)} async-done(((f32[1280,1280]{1,0:T(8,128)}), f32[40,1280]{1,0:T(8,128)}) %reduce-scatter.20.cloned.1.call-update) | async-done | bytes 204816 | tf_op jit(solution)/shard_map/reduce_scatter | solution.py:316
  (568 shorter events, 136.6 us)
Async XLA Ops:
  7.2 239.4 %all-gather.5.cloned.1.call-start = ((), (), s32[]{:S(2)}) async-start(), calls=%async_computation.7 | async-start | bytes 2027520 | tf_op jit(solution)/shard_map/all_gather | solution.py:102
  7.9 280.6 %all-gather.7.cloned.1.call-start = ((), (), s32[]{:S(2)}) async-start(), calls=%async_computation.8 | async-start | bytes 3379200 | tf_op jit(solution)/shard_map/all_gather | solution.py:103
  8.7 287.6 %all-gather.9.cloned.1.call-start = ((), (), s32[]{:S(2)}) async-start(), calls=%async_computation.9 | async-start | bytes 3379200 | tf_op jit(solution)/shard_map/all_gather | solution.py:106
  9.4 304.0 %all-gather.11.cloned.1.call-start = ((), (), s32[]{:S(2)}) async-start(), calls=%async_computation.10 | async-start | bytes 3379200 | tf_op jit(solution)/shard_map/all_gather | solution.py:107
  9.4 199.0 %collective-permute-start = (bf16[1,24,256]{2,1,0:T(8,128)(2,1)}, bf16[1,24,256]{2,1,0:T(8,128)(2,1)S(1)}, u32[]{:S(2)}, u32[]{:S(2)}) collective-permute-start(bf16[1,24,256]{2,1,0:T(8,128)(2,1)} %bitcast.373), channel_id=1, source_target_pairs={{0,1},{1,0},{2,3},{3,2},{4,5},{5,4},{6,7},{7,6},{8,9},{9,8},{10,11... | collective-permute-start | bytes 36872 | tf_op jit(solution)/shard_map/ppermute | solution.py:27
  12.5 601.7 %reduce-scatter.12.cloned.1.call-start = ((), (), s32[]{:S(2)}) async-start(), calls=%async_computation.12 | async-start | bytes 811008 | tf_op jit(solution)/shard_map/reduce_scatter | solution.py:310
  57.7 328.8 %copy-start.100 = (f32[768]{0:T(1024)}, f32[768]{0:T(1024)S(1)}, u32[]{:S(2)}) copy-start(f32[768]{0:T(1024)S(1)} %convert_element_type.339) | copy-start | bytes 9220
  57.7 183.1 %copy-start.118 = (f32[768]{0:T(1024)}, f32[768]{0:T(1024)S(1)}, u32[]{:S(2)}) copy-start(f32[768]{0:T(1024)S(1)} %convert_element_type.340) | copy-start | bytes 9220
  60.9 185.7 %copy-start.88 = (f32[1024]{0:T(1024)}, f32[1024]{0:T(1024)S(1)}, u32[]{:S(2)}) copy-start(f32[1024]{0:T(1024)S(1)} %broadcast_multiply_fusion.2) | copy-start | bytes 12292
  61.0 324.0 %copy-start.106 = (f32[1024]{0:T(1024)}, f32[1024]{0:T(1024)S(1)}, u32[]{:S(2)}) copy-start(f32[1024]{0:T(1024)S(1)} %get-tuple-element.197) | copy-start | bytes 12292
  61.0 325.5 %copy-start.104 = (f32[1024]{0:T(1024)}, f32[1024]{0:T(1024)S(1)}, u32[]{:S(2)}) copy-start(f32[1024]{0:T(1024)S(1)} %get-tuple-element.196) | copy-start | bytes 12292
  63.4 141.4 %copy-start.96 = (f32[1024]{0:T(1024)}, f32[1024]{0:T(1024)S(1)}, u32[]{:S(2)}) copy-start(f32[1024]{0:T(1024)S(1)} %get-tuple-element.72) | copy-start | bytes 12292
  63.4 157.9 %copy-start.98 = (f32[1024]{0:T(1024)}, f32[1024]{0:T(1024)S(1)}, u32[]{:S(2)}) copy-start(f32[1024]{0:T(1024)S(1)} %get-tuple-element.71) | copy-start | bytes 12292
  63.4 183.2 %copy-start.102 = (f32[1024]{0:T(1024)}, f32[1024]{0:T(1024)S(1)}, u32[]{:S(2)}) copy-start(f32[1024]{0:T(1024)S(1)} %fusion.160) | copy-start | bytes 12292
  63.5 143.7 %copy-start.74 = (f32[1280]{0:T(1024)}, f32[1280]{0:T(1024)S(1)}, u32[]{:S(2)}) copy-start(f32[1280]{0:T(1024)S(1)} %convert_element_type.343) | copy-start | bytes 15364
  64.0 143.1 %copy-start.76 = (f32[1280]{0:T(1024)}, f32[1280]{0:T(1024)S(1)}, u32[]{:S(2)}) copy-start(f32[1280]{0:T(1024)S(1)} %convert_element_type.344) | copy-start | bytes 15364
  64.0 71.6 %copy-start.117 = (bf16[40,256]{1,0:T(8,128)(2,1)S(1)}, bf16[40,256]{1,0:T(8,128)(2,1)}, u32[]{:S(2)}) copy-start(bf16[40,256]{1,0:T(8,128)(2,1)} %param.23) | copy-start | bytes 61444
  135.3 71.9 %copy-start.86 = (f32[256]{0:T(256)}, f32[256]{0:T(256)S(1)}, u32[]{:S(2)}) copy-start(f32[256]{0:T(256)S(1)} %broadcast_multiply_fusion.6) | copy-start | bytes 3076
  135.6 69.2 %copy-start.147 = (f32[256]{0:T(256)}, f32[256]{0:T(256)S(1)}, u32[]{:S(2)}) copy-start(f32[256]{0:T(256)S(1)} %fusion.101) | copy-start | bytes 3076
  135.6 71.5 %copy-start.92 = (f32[256]{0:T(256)}, f32[256]{0:T(256)S(1)}, u32[]{:S(2)}) copy-start(f32[256]{0:T(256)S(1)} %fusion.163) | copy-start | bytes 3076
  204.8 30.1 %copy-start.136 = (f32[1024]{0:T(1024)}, f32[1024]{0:T(1024)S(1)}, u32[]{:S(2)}) copy-start(f32[1024]{0:T(1024)S(1)} %fusion.161) | copy-start | bytes 12292
  208.5 4.0 collective-permute-start.1
  209.2 22.4 %copy-start.121 = (pred[1024]{0:T(1024)(128)(4,1)}, pred[1024]{0:T(1024)(128)(4,1)S(1)}, u32[]{:S(2)}) copy-start(pred[1024]{0:T(1024)(128)(4,1)S(1)} %iota_compare_fusion.2) | copy-start | bytes 3076
  212.5 5.2 collective-permute-start.2
  213.2 24.3 %copy-start.124 = (pred[1024]{0:T(1024)(128)(4,1)}, pred[1024]{0:T(1024)(128)(4,1)S(1)}, u32[]{:S(2)}) copy-start(pred[1024]{0:T(1024)(128)(4,1)S(1)} %iota_compare_fusion.1) | copy-start | bytes 3076
  213.3 95.0 %copy-start.78 = (f32[1280]{0:T(1024)}, f32[1280]{0:T(1024)S(1)}, u32[]{:S(2)}) copy-start(f32[1280]{0:T(1024)S(1)} %convert_element_type.355) | copy-start | bytes 15364
  217.8 1.4 collective-permute-start.3
  218.5 24.8 %copy-start.127 = (pred[1024]{0:T(1024)(128)(4,1)}, pred[1024]{0:T(1024)(128)(4,1)S(1)}, u32[]{:S(2)}) copy-start(pred[1024]{0:T(1024)(128)(4,1)S(1)} %iota_compare_fusion) | copy-start | bytes 3076
  219.2 10.2 collective-permute-start.4
  221.3 165.2 %copy-start.139 = (f32[1024]{0:T(1024)}, f32[1024]{0:T(1024)S(1)}, u32[]{:S(2)}) copy-start(f32[1024]{0:T(1024)S(1)} %fusion.162) | copy-start | bytes 12292
  235.0 109.3 %copy-start.82 = (f32[8,256]{1,0:T(8,128)}, f32[8,256]{1,0:T(8,128)S(1)}, u32[]{:S(2)}) copy-start(f32[8,256]{1,0:T(8,128)S(1)} %log_add_fusion.2) | copy-start | bytes 24580
  240.8 120.7 %copy-start.84 = (f32[8,256]{1,0:T(8,128)}, f32[8,256]{1,0:T(8,128)S(1)}, u32[]{:S(2)}) copy-start(f32[8,256]{1,0:T(8,128)S(1)} %log_add_fusion.1) | copy-start | bytes 24580
  246.6 132.2 %copy-start.80 = (f32[8,256]{1,0:T(8,128)}, f32[8,256]{1,0:T(8,128)S(1)}, u32[]{:S(2)}) copy-start(f32[8,256]{1,0:T(8,128)S(1)} %log_add_fusion) | copy-start | bytes 24580
  291.9 35.9 %copy-start.114 = (f32[256]{0:T(256)}, f32[256]{0:T(256)S(1)}, u32[]{:S(2)}) copy-start(f32[256]{0:T(256)S(1)} %broadcast_multiply_fusion.5) | copy-start | bytes 3076
  293.4 34.5 %copy-start.130 = (f32[256]{0:T(256)}, f32[256]{0:T(256)S(1)}, u32[]{:S(2)}) copy-start(f32[256]{0:T(256)S(1)} %broadcast_multiply_fusion.4) | copy-start | bytes 3076
  294.8 33.1 %copy-start.132 = (f32[256]{0:T(256)}, f32[256]{0:T(256)S(1)}, u32[]{:S(2)}) copy-start(f32[256]{0:T(256)S(1)} %broadcast_multiply_fusion.3) | copy-start | bytes 3076
  296.2 31.7 %copy-start.134 = (f32[256]{0:T(256)}, f32[256]{0:T(256)S(1)}, u32[]{:S(2)}) copy-start(f32[256]{0:T(256)S(1)} %fusion.164) | copy-start | bytes 3076
  296.2 31.7 %copy-start.151 = (f32[256]{0:T(256)}, f32[256]{0:T(256)S(1)}, u32[]{:S(2)}) copy-start(f32[256]{0:T(256)S(1)} %fusion.165) | copy-start | bytes 3076
  296.2 31.7 %copy-start.149 = (f32[256]{0:T(256)}, f32[256]{0:T(256)S(1)}, u32[]{:S(2)}) copy-start(f32[256]{0:T(256)S(1)} %fusion.166) | copy-start | bytes 3076
  388.6 231.6 %reduce-scatter.10.cloned.1.call-start = ((), (), s32[]{:S(2)}) async-start(), calls=%async_computation.11 | async-start | bytes 1351680 | tf_op jit(solution)/shard_map/reduce_scatter | solution.py:309
  399.5 356.4 %reduce-scatter.22.cloned.1.call-start = ((), (), s32[]{:S(2)}) async-start(), calls=%async_computation.17 | async-start | bytes 1351680
  423.4 439.0 %reduce-scatter.14.cloned.1.call-start = ((), (), s32[]{:S(2)}) async-start(), calls=%async_computation.13 | async-start | bytes 4055040 | tf_op jit(solution)/shard_map/reduce_scatter | solution.py:311
  442.2 574.8 %reduce-scatter.18.cloned.1.call-start = ((), (), s32[]{:S(2)}) async-start(), calls=%async_computation.15 | async-start | bytes 6758400 | tf_op jit(solution)/shard_map/reduce_scatter | solution.py:315
  450.3 720.3 %reduce-scatter.16.cloned.1.call-start = ((), (), s32[]{:S(2)}) async-start(), calls=%async_computation.14 | async-start | bytes 6758400 | tf_op jit(solution)/shard_map/reduce_scatter | solution.py:312
  457.9 868.4 %reduce-scatter.20.cloned.1.call-start = ((), (), s32[]{:S(2)}) async-start(), calls=%async_computation.16 | async-start | bytes 6758400 | tf_op jit(solution)/shard_map/reduce_scatter | solution.py:316
  548.2 49.6 %copy-start.99 = (f32[1024]{0:T(1024)S(1)}, f32[1024]{0:T(1024)}, u32[]{:S(2)}) copy-start(f32[1024]{0:T(1024)} %copy-done.98) | copy-start | bytes 12292
  548.3 49.6 %copy-start.97 = (f32[1024]{0:T(1024)S(1)}, f32[1024]{0:T(1024)}, u32[]{:S(2)}) copy-start(f32[1024]{0:T(1024)} %copy-done.96) | copy-start | bytes 12292
  548.3 49.6 %copy-start.95 = (f32[1024]{0:T(1024)S(1)}, f32[1024]{0:T(1024)}, u32[]{:S(2)}) copy-start(f32[1024]{0:T(1024)} %copy-done.94) | copy-start | bytes 12292
  (159 other events, 578.7 us)
Sparse Core Ops, SparseCore 0:
  10.9 58.9 all-gather.4
  72.8 59.8 all-gather.6
  135.5 59.2 all-gather.8
  197.5 58.5 all-gather.10
  388.7 93.9 reduce-scatter.11
  485.4 134.7 reduce-scatter.9
  623.1 132.7 reduce-scatter.21
  761.9 100.5 reduce-scatter.13
  865.3 151.6 reduce-scatter.17
  1019.7 150.8 reduce-scatter.15
  1173.5 152.7 reduce-scatter.19
